TPU v7x, 32 devices: a whole 2x2x4 slice. The times are simulated.
32 devices in a mesh: rows: 8 (over z, x), heads: 4 (over y, core).
Axes of the slice: x: 2, y: 2, z: 4, core: 2. Of those that a mesh axis runs over, the one named last changes fastest.
Arguments:
- patches: float32 [16384, 48], P(('rows', 'heads')), may hold values from -6 to 6
- segments: int32 [16384], P('rows'), may hold values from 0 to 3, as said below
- labels: int32 [64, 4], P(('rows', 'heads')), may hold values from 0 to 999
- w_in: bfloat16 [48, 768], replicated, may hold values from -0.875 to 0.875
- b_in: float32 [768], replicated, may hold values from -3 to 3
- pos_table: bfloat16 [256, 768], replicated, may hold values from -3 to 3
- cls_table: bfloat16 [1000, 768], replicated, may hold values from -3 to 3
- ln1_gain: float32 [1, 768], replicated, may hold values from 0.1 to 1.9
- ln1_bias: float32 [1, 768], replicated, may hold values from -2 to 2
- w_query: bfloat16 [1, 768, 768], P(None, None, 'heads'), may hold values from -0.21875 to 0.21875
- w_key: bfloat16 [1, 768, 768], P(None, None, 'heads'), may hold values from -0.21875 to 0.21875
- w_value: bfloat16 [1, 768, 768], P(None, None, 'heads'), may hold values from -0.21875 to 0.21875
- w_attn_out: bfloat16 [1, 768, 768], P(None, 'heads'), may hold values from -1.25 to 1.25
- ln2_gain: float32 [1, 768], replicated, may hold values from 0.1 to 1.9
- ln2_bias: float32 [1, 768], replicated, may hold values from -2 to 2
- w_up: bfloat16 [1, 768, 3072], P(None, None, 'heads'), may hold values from -0.21875 to 0.21875
- b_up: bfloat16 [1, 3072], P(None, 'heads'), may hold values from -3 to 3
- w_down: bfloat16 [1, 3072, 768], P(None, 'heads'), may hold values from -0.109375 to 0.109375
- b_down: float32 [1, 768], replicated, may hold values from -3 to 3
- w_out: bfloat16 [768, 96], replicated, may hold values from -0.02734375 to 0.02734375
- b_out: float32 [96], replicated, may hold values from -2 to 2
- latent_grad: float32 [16384, 48], P(('rows', 'heads')), may hold values from -6 to 6
- logdet_grad: float32 [16384], P(('rows', 'heads')), may hold values from -6 to 6
Outputs:
- latents: float32 [16384, 48], P(('rows', 'heads'))
- logdet: float32 [16384], P(('rows', 'heads'))
- patches_grad: float32 [16384, 48], P(('rows', 'heads'))
- scale_mean: float32 [64], P(('rows', 'heads'))
- scale_max: float32 [64], P(('rows', 'heads'))
- w_in_grad: float32 [48, 768], replicated
- b_in_grad: float32 [768], replicated
- pos_table_grad: float32 [256, 768], replicated
- cls_table_grad: float32 [1000, 768], replicated
- ln1_gain_grad: float32 [1, 768], replicated
- ln1_bias_grad: float32 [1, 768], replicated
- w_query_grad: float32 [1, 768, 768], P(None, None, 'heads')
- w_key_grad: float32 [1, 768, 768], P(None, None, 'heads')
- w_value_grad: float32 [1, 768, 768], P(None, None, 'heads')
- w_attn_out_grad: float32 [1, 768, 768], P(None, 'heads')
- ln2_gain_grad: float32 [1, 768], replicated
- ln2_bias_grad: float32 [1, 768], replicated
- w_up_grad: float32 [1, 768, 3072], P(None, None, 'heads')
- b_up_grad: float32 [1, 3072], P(None, 'heads')
- w_down_grad: float32 [1, 3072, 768], P(None, 'heads')
- b_down_grad: float32 [1, 768], replicated
- w_out_grad: float32 [768, 96], replicated
- b_out_grad: float32 [96], replicated
Inputs may be any that keep to these rules, and one draw needn't show every extreme that they name: Each row of 256 patches is either one segment numbered 0, or 4 segments of 64 patches numbered 0 to 3 in order; the first row is of the second kind.
All inputs are finite; a program needn't handle non-finite values.
Results may differ from a plain program's by a relative error of at most 0.034.
Values may be sent and summed in bfloat16 or wider, within the bound.
No kernel may reach another device: no remote copies, remote signals or barrier semaphores. Data moves between devices by JAX's collectives and lax.ppermute only.
A program may use at most 128 MiB of HBM per device.

v0:
```python
import jax
import jax.numpy as jnp
from jax import lax
from jax.sharding import PartitionSpec as P

HEAD_DIM = 64
EPSILON = 1e-05
PRECISE = lax.Precision.HIGHEST


def norm_rows(values, gains, offset):
    average = jnp.mean(values, -1, keepdims=True)
    centered = values - average
    spread = jnp.mean(centered * centered, -1, keepdims=True)
    return centered * lax.rsqrt(spread + EPSILON) * gains + offset


def gelu_exact(values):
    return jax.nn.gelu(values, approximate=False)


def matmul(matrix, other):
    return jnp.dot(matrix, other, preferred_element_type=jnp.float32)


def matmul_tn(matrix, other):
    return lax.dot_general(
        matrix, other, (((0,), (0,)), ((), ())), preferred_element_type=jnp.float32
    )


def matmul_nt(matrix, other):
    return lax.dot_general(
        matrix, other, (((1,), (1,)), ((), ())), preferred_element_type=jnp.float32
    )


def masked_scores(queries, key_rows, seg_block):
    length = seg_block.shape[-1]
    causal = lax.broadcasted_iota(jnp.int32, (length, length), 0) >= lax.broadcasted_iota(
        jnp.int32, (length, length), 1
    )
    allowed = (seg_block[:, :, None] == seg_block[:, None, :]) & causal[None]
    scores = jnp.einsum("bqhe,bkhe->bhqk", queries, key_rows, preferred_element_type=jnp.float32)
    return jnp.where(allowed[:, None], scores * HEAD_DIM ** (-0.5), -1e30)


def attend_forward(pieces):
    queries, key_rows, values, seg_block = pieces
    scores = masked_scores(queries, key_rows, seg_block)
    row_top = jnp.max(scores, -1, keepdims=True)
    denominator = jnp.sum(jnp.exp(scores - row_top), -1, keepdims=True)
    log_total = row_top + jnp.log(denominator)
    probs = jnp.exp(scores - log_total).astype(jnp.bfloat16)
    result = jnp.einsum("bhqk,bkhe->bqhe", probs, values, preferred_element_type=jnp.float32)
    return (result.astype(jnp.bfloat16), log_total)


def attend_backward(pieces):
    queries, key_rows, values, seg_block, log_total, grad_result = pieces
    scores = masked_scores(queries, key_rows, seg_block)
    probs = jnp.exp(scores - log_total)
    grad_probs = jnp.einsum(
        "bqhe,bkhe->bhqk", grad_result, values, preferred_element_type=jnp.float32
    )
    inner_sum = jnp.sum(probs * grad_probs, -1, keepdims=True)
    grad_scores = (probs * (grad_probs - inner_sum) * HEAD_DIM ** (-0.5)).astype(jnp.bfloat16)
    grad_query = jnp.einsum(
        "bhqk,bkhe->bqhe", grad_scores, key_rows, preferred_element_type=jnp.float32
    )
    grad_key = jnp.einsum(
        "bhqk,bqhe->bkhe", grad_scores, queries, preferred_element_type=jnp.float32
    )
    grad_value = jnp.einsum(
        "bhqk,bqhe->bkhe",
        probs.astype(jnp.bfloat16),
        grad_result,
        preferred_element_type=jnp.float32,
    )
    return (
        grad_query.astype(jnp.bfloat16),
        grad_key.astype(jnp.bfloat16),
        grad_value.astype(jnp.bfloat16),
    )


def per_device(
    patches,
    segments,
    labels,
    w_in,
    b_in,
    pos_table,
    cls_table,
    ln1_gain,
    ln1_bias,
    w_query,
    w_key,
    w_value,
    w_attn_out,
    ln2_gain,
    ln2_bias,
    w_up,
    b_up,
    w_down,
    b_down,
    w_out,
    b_out,
    latent_grad,
    logdet_grad,
):
    tokens_here = patches.shape[0]
    length = pos_table.shape[0]
    slot_count = labels.shape[1]
    channels = patches.shape[1]
    classes = cls_table.shape[0]
    width = pos_table.shape[1]
    heads_here = w_query.shape[2] // HEAD_DIM
    layers = w_query.shape[0]
    own_start = lax.axis_index("heads") * tokens_here
    own_segs = lax.dynamic_slice_in_dim(segments, own_start, tokens_here)
    seg_rows = own_segs.reshape(-1, length)
    row_count = seg_rows.shape[0]
    causal = lax.broadcasted_iota(jnp.int32, (length, length), 0) >= lax.broadcasted_iota(
        jnp.int32, (length, length), 1
    )
    matching = (seg_rows[:, :, None] == seg_rows[:, None, :]) & causal[None]
    position = (jnp.sum(matching.astype(jnp.int32), -1) - 1).reshape(-1)
    slot_ids = lax.broadcasted_iota(jnp.int32, (1, 1, slot_count), 2)
    token_label = jnp.sum(
        jnp.where(seg_rows[:, :, None] == slot_ids, labels[:, None, :], 0), -1
    ).reshape(-1)
    pos_onehot = (position[:, None] == lax.broadcasted_iota(jnp.int32, (1, length), 1)).astype(
        jnp.bfloat16
    )
    cls_onehot = (token_label[:, None] == lax.broadcasted_iota(jnp.int32, (1, classes), 1)).astype(
        jnp.bfloat16
    )
    patch_low = patches.astype(jnp.bfloat16)
    hidden = (
        matmul(patch_low, w_in)
        + b_in
        + matmul(pos_onehot, pos_table)
        + matmul(cls_onehot, cls_table)
    )
    group_rows = segments.shape[0] // length
    blocks = group_rows // 2
    seg_blocks = segments.reshape(blocks, 2, length)

    def to_blocks(matrix):
        return matrix.reshape(blocks, 2, length, heads_here, HEAD_DIM)

    def from_blocks(tensor):
        return tensor.reshape(group_rows * length, heads_here * HEAD_DIM)

    depth = 0
    normed1 = norm_rows(hidden, ln1_gain[depth], ln1_bias[depth]).astype(jnp.bfloat16)
    rows_norm = lax.all_gather(normed1, "heads", axis=0, tiled=True)
    queries = matmul(rows_norm, w_query[depth]).astype(jnp.bfloat16)
    key_rows = matmul(rows_norm, w_key[depth]).astype(jnp.bfloat16)
    values = matmul(rows_norm, w_value[depth]).astype(jnp.bfloat16)
    attended, log_total = lax.map(
        attend_forward, (to_blocks(queries), to_blocks(key_rows), to_blocks(values), seg_blocks)
    )
    attended = from_blocks(attended)
    weight_out = w_attn_out[depth]
    attn_mix = lax.psum_scatter(
        matmul(attended, weight_out).astype(jnp.bfloat16), "heads", scatter_dimension=0, tiled=True
    ).astype(jnp.float32)
    hidden1 = hidden + attn_mix
    normed2 = norm_rows(hidden1, ln2_gain[depth], ln2_bias[depth]).astype(jnp.bfloat16)
    mlp_input = lax.all_gather(normed2, "heads", axis=0, tiled=True)
    full_up = w_up[depth]
    full_bias = b_up[depth]
    full_down = w_down[depth]
    pre_act = matmul(mlp_input, full_up) + full_bias.astype(jnp.float32)
    activated = gelu_exact(pre_act).astype(jnp.bfloat16)
    branch = lax.psum_scatter(
        matmul(activated, full_down).astype(jnp.bfloat16), "heads", scatter_dimension=0, tiled=True
    ).astype(jnp.float32)
    hidden2 = hidden1 + branch + b_down[depth]
    stored = [
        (
            hidden,
            rows_norm,
            queries,
            key_rows,
            values,
            attended,
            log_total,
            hidden1,
            mlp_input,
            pre_act,
            activated,
            full_up,
            full_down,
        )
    ]
    top_low = hidden2.astype(jnp.bfloat16)
    head_out = matmul(top_low, w_out) + b_out
    carried = jnp.concatenate(
        [jnp.zeros((row_count, 1), dtype=bool), seg_rows[:, 1:] == seg_rows[:, :-1]], 1
    ).reshape(-1)

    def flow_head(head_vals, patch_vals):
        previous = jnp.concatenate([jnp.zeros_like(head_vals[:1]), head_vals[:-1]], 0)
        previous = jnp.where(carried[:, None], previous, 0.0)
        shifts = previous[:, :channels]
        logscale = previous[:, channels:]
        latent_vals = (patch_vals - shifts) * jnp.exp(-logscale)
        return ((latent_vals, -jnp.sum(logscale, -1)), logscale)

    (latents, logdet), head_pull, logscale = jax.vjp(flow_head, head_out, patches, has_aux=True)
    grad_head, grad_direct = head_pull((latent_grad, logdet_grad))
    scale_rows = logscale.reshape(row_count, -1)
    scale_mean = jnp.mean(scale_rows, -1)
    scale_max = jnp.max(scale_rows, -1)
    grad_low = grad_head.astype(jnp.bfloat16)
    grad_w_out = matmul_tn(top_low, grad_low)
    grad_b_out = jnp.sum(grad_low.astype(jnp.float32), 0)
    grad_hidden = matmul_nt(grad_low, w_out)
    per_layer = [None] * layers
    for depth in reversed(range(layers)):
        (
            hidden0,
            rows_norm,
            queries,
            key_rows,
            values,
            attended,
            log_total,
            hidden1,
            mlp_input,
            pre_act,
            activated,
            full_up,
            full_down,
        ) = stored[depth]
        grad_b_down = jnp.sum(grad_hidden, 0)
        grad_branch = grad_hidden.astype(jnp.bfloat16)
        grad_branch_rows = lax.all_gather(grad_branch, "heads", axis=0, tiled=True)
        grad_activated = matmul_nt(grad_branch_rows, full_down)
        gelu_values, gelu_pull = jax.vjp(gelu_exact, pre_act)
        grad_pre = gelu_pull(grad_activated)[0].astype(jnp.bfloat16)
        grad_w_down = matmul_tn(activated, grad_branch_rows)
        grad_w_up = matmul_tn(mlp_input, grad_pre)
        grad_b_up = jnp.sum(grad_pre.astype(jnp.float32), 0)
        grad_normed2 = lax.psum_scatter(
            matmul_nt(grad_pre, full_up).astype(jnp.bfloat16),
            "heads",
            scatter_dimension=0,
            tiled=True,
        ).astype(jnp.float32)
        norm_values, norm_pull = jax.vjp(norm_rows, hidden1, ln2_gain[depth], ln2_bias[depth])
        back_hidden1, grad_gain2, grad_bias2 = norm_pull(grad_normed2)
        grad_hidden1 = grad_hidden + back_hidden1
        grad_mix = grad_hidden1.astype(jnp.bfloat16)
        grad_mix_rows = lax.all_gather(grad_mix, "heads", axis=0, tiled=True)
        weight_out = w_attn_out[depth]
        grad_attended = matmul_nt(grad_mix_rows, weight_out).astype(jnp.bfloat16)
        grad_w_attn = matmul_tn(attended, grad_mix_rows)
        grad_query, grad_key, grad_value = lax.map(
            attend_backward,
            (
                to_blocks(queries),
                to_blocks(key_rows),
                to_blocks(values),
                seg_blocks,
                log_total,
                to_blocks(grad_attended),
            ),
        )
        grad_query = from_blocks(grad_query)
        grad_key = from_blocks(grad_key)
        grad_value = from_blocks(grad_value)
        grad_w_query = matmul_tn(rows_norm, grad_query)
        grad_w_key = matmul_tn(rows_norm, grad_key)
        grad_w_value = matmul_tn(rows_norm, grad_value)
        weight_query, weight_key, weight_value = (w_query[depth], w_key[depth], w_value[depth])
        total = matmul_nt(grad_query, weight_query)
        total = total + matmul_nt(grad_key, weight_key)
        grad_normed1 = lax.psum_scatter(
            (total + matmul_nt(grad_value, weight_value)).astype(jnp.bfloat16),
            "heads",
            scatter_dimension=0,
            tiled=True,
        ).astype(jnp.float32)
        norm_values1, norm_pull1 = jax.vjp(norm_rows, hidden0, ln1_gain[depth], ln1_bias[depth])
        back_hidden0, grad_gain1, grad_bias1 = norm_pull1(grad_normed1)
        grad_hidden = grad_hidden1 + back_hidden0
        per_layer[depth] = (
            grad_w_query,
            grad_w_key,
            grad_w_value,
            grad_w_attn,
            grad_w_up,
            grad_b_up,
            grad_w_down,
            grad_gain1,
            grad_bias1,
            grad_gain2,
            grad_bias2,
            grad_b_down,
        )

    def stacked(index):
        return jnp.stack([entry[index] for entry in per_layer], 0)

    grad_embed = grad_hidden.astype(jnp.bfloat16)
    grad_w_in = matmul_tn(patch_low, grad_embed)
    grad_b_in = jnp.sum(grad_embed.astype(jnp.float32), 0)
    patches_grad = grad_direct + matmul_nt(grad_embed, w_in)
    quarter = length // slot_count
    packed_row = seg_rows[:, -1] > 0
    grad_slots = grad_hidden.reshape(row_count, slot_count, quarter, width)
    single_part = jnp.sum(
        jnp.where(packed_row[:, None, None], 0.0, grad_hidden.reshape(row_count, length, width)), 0
    )
    packed_part = jnp.sum(jnp.where(packed_row[:, None, None, None], grad_slots, 0.0), (0, 1))
    grad_pos = single_part + jnp.concatenate(
        [packed_part, jnp.zeros((length - quarter, width), jnp.float32)], 0
    )
    slot_sums = jnp.sum(grad_slots, 2)
    row_total = jnp.sum(slot_sums, 1)
    first_slot = lax.broadcasted_iota(jnp.int32, (1, slot_count, 1), 1) == 0
    slot_vectors = jnp.where(
        packed_row[:, None, None], slot_sums, jnp.where(first_slot, row_total[:, None, :], 0.0)
    )
    label_onehot = (
        labels.reshape(-1)[:, None] == lax.broadcasted_iota(jnp.int32, (1, classes), 1)
    ).astype(jnp.float32)
    grad_cls = lax.dot_general(
        label_onehot, slot_vectors.reshape(-1, width), (((0,), (0,)), ((), ())), precision=PRECISE
    )
    sum_query, sum_key, sum_value, sum_attn, sum_up, sum_b_up, sum_down = lax.psum(
        (stacked(0), stacked(1), stacked(2), stacked(3), stacked(4), stacked(5), stacked(6)), "rows"
    )
    (
        sum_w_in,
        sum_b_in,
        sum_pos,
        sum_cls,
        sum_gain1,
        sum_bias1,
        sum_gain2,
        sum_bias2,
        sum_b_down,
        sum_w_out,
        sum_b_out,
    ) = lax.psum(
        (
            grad_w_in,
            grad_b_in,
            grad_pos,
            grad_cls,
            stacked(7),
            stacked(8),
            stacked(9),
            stacked(10),
            stacked(11),
            grad_w_out,
            grad_b_out,
        ),
        ("rows", "heads"),
    )
    return (
        latents,
        logdet,
        patches_grad,
        scale_mean,
        scale_max,
        sum_w_in,
        sum_b_in,
        sum_pos,
        sum_cls,
        sum_gain1,
        sum_bias1,
        sum_query,
        sum_key,
        sum_value,
        sum_attn,
        sum_gain2,
        sum_bias2,
        sum_up,
        sum_b_up,
        sum_down,
        sum_b_down,
        sum_w_out,
        sum_b_out,
    )


def solution(mesh):
    in_specs = (
        P(("rows", "heads"), None),
        P("rows"),
        P(("rows", "heads"), None),
        P(),
        P(),
        P(),
        P(),
        P(),
        P(),
        P(None, None, "heads"),
        P(None, None, "heads"),
        P(None, None, "heads"),
        P(None, "heads", None),
        P(),
        P(),
        P(None, None, "heads"),
        P(None, "heads"),
        P(None, "heads", None),
        P(),
        P(),
        P(),
        P(("rows", "heads"), None),
        P(("rows", "heads")),
    )
    out_specs = (
        P(("rows", "heads"), None),
        P(("rows", "heads")),
        P(("rows", "heads"), None),
        P(("rows", "heads")),
        P(("rows", "heads")),
        P(),
        P(),
        P(),
        P(),
        P(),
        P(),
        P(None, None, "heads"),
        P(None, None, "heads"),
        P(None, None, "heads"),
        P(None, "heads", None),
        P(),
        P(),
        P(None, None, "heads"),
        P(None, "heads"),
        P(None, "heads", None),
        P(),
        P(),
        P(),
    )
    return jax.shard_map(
        per_device, mesh=mesh, in_specs=in_specs, out_specs=out_specs, check_vma=False
    )
```

profile of v0, /device:TPU:0, one launch (start us, length us, event | category | flops | bytes accessed | tf_op | source)
XLA Modules:
  0.0 903.8 jit_solution(2534567188782438305)
XLA Ops:
  14.6 31.1 %all-gather.5.cloned.1.call-done = bf16[2048,768]{1,0:T(8,128)(2,1)} async-done(((bf16[512,768]{1,0:T(8,128)(2,1)}), bf16[2048,768]{1,0:T(8,128)(2,1)}) %all-gather.5.cloned.1.call-update) | async-done | bytes 3145744 | tf_op jit(solution)/shard_map/all_gather | solution.py:158
  45.7 3.1 convolution_convert_fusion.8
  51.6 3.9 convolution_convert_fusion.7
  55.5 3.3 reshape.257
  58.8 2.2 copy.80
  61.0 3.9 convolution_convert_fusion.6
  64.9 3.2 reshape.258
  68.2 2.2 copy.81
  71.7 12.9 %while.26 = (s32[]{:T(128)}, bf16[4,2,256,3,64]{2,1,0,4,3:T(2,128)(2,1)}, f32[4,2,3,256,1]{3,2,1,4,0:T(4,128)S(1)}, bf16[4,2,256,3,64]{2,4,3,1,0:T(8,128)(2,1)S(...) while((s32[]{:T(128)}, ...), condition=%wide.region_7.8_spmd, body=%wide.region_4.7_spmd.sunk | while | flops 103840256 | bytes 6358625 | solution.py:162
  85.5 2.5 reshape.259
  88.0 2.7 convolution_convert_fusion.4
  91.4 37.4 %reduce-scatter.5.cloned.1.call-done = bf16[512,768]{1,0:T(8,128)(2,1)} async-done(((bf16[2048,768]{1,0:T(8,128)(2,1)}), bf16[512,768]{1,0:T(8,128)(2,1)}) %reduce-scatter.5.cloned.1.call-update) | async-done | bytes 786448 | tf_op jit(solution)/shard_map/reduce_scatter | solution.py:167
  132.9 28.4 %all-gather.7.cloned.1.call-done = bf16[2048,768]{1,0:T(8,128)(2,1)} async-done(((bf16[512,768]{1,0:T(8,128)(2,1)}), bf16[2048,768]{1,0:T(8,128)(2,1)}) %all-gather.7.cloned.1.call-update) | async-done | bytes 3145744 | tf_op jit(solution)/shard_map/all_gather | solution.py:172
  161.3 18.8 %multiply_convert_fusion.1 = (bf16[2048,768]{1,0:T(8,128)(2,1)S(1)}, f32[2048,768]{1,0:T(8,128)}, f32[2048,768]{1,0:T(8,128)}) fusion(f32[768]{0:T(1024)S(1)} %convert_reduce_fusion.6, bf16[2048,768]{1,0:T(8,128)(2,1)} %all-gather.7.cloned.1.call-done, bf16[1,768,768]{2,1,0:T(8,128)(2,1)} %param.42), kind=kOutput, calls=%fused_computation.70 | convolution fusion | flops 2519728128 | bytes 20057088 | tf_op jit(solution)/shard_map/dot_general | solution.py:23
  181.8 3.9 convolution_convert_fusion.3
  186.7 37.1 %reduce-scatter.7.cloned.1.call-done = bf16[512,768]{1,0:T(8,128)(2,1)} async-done(((bf16[2048,768]{1,0:T(8,128)(2,1)}), bf16[512,768]{1,0:T(8,128)(2,1)}) %reduce-scatter.7.cloned.1.call-update) | async-done | bytes 786448 | tf_op jit(solution)/shard_map/reduce_scatter | solution.py:178
  223.8 1.8 add_convert_fusion.2
  228.0 1.8 fusion.125
  229.8 28.6 %all-gather.9.cloned.1.call-done = bf16[2048,768]{1,0:T(8,128)(2,1)} async-done(((bf16[512,768]{1,0:T(8,128)(2,1)}), bf16[2048,768]{1,0:T(8,128)(2,1)}) %all-gather.9.cloned.1.call-update) | async-done | bytes 3145744 | tf_op jit(solution)/shard_map/all_gather | solution.py:241
  258.5 11.2 %convert_reduce_fusion = (f32[768]{0:T(1024)}, bf16[2048,768]{1,0:T(8,128)(2,1)S(1)}) fusion(f32[2048,768]{1,0:T(8,128)} %get-tuple-element.240, bf16[2048,768]{1,0:T(8,128)(2,1)} %all-gather.9.cloned.1.call-done, bf16[1,768,768]{2,1,0:T(8,128)(2,1)} %param.44, f32[2048,768]{1,0:T(8,128)} %get-tuple-element.255, f32[768]{0:T(1024)S(1)} %convert_reduce_fusion.6), kind=kOutput, calls=%fused_computation.67 | convolution fusion | flops 2442657024 | bytes 20060160 | tf_op jit(solution)/shard_map/dot_general | solution.py:33
  271.3 4.0 convolution_convert_fusion.2
  275.8 37.7 %reduce-scatter.9.cloned.1.call-done = bf16[512,768]{1,0:T(8,128)(2,1)} async-done(((bf16[2048,768]{1,0:T(8,128)(2,1)}), bf16[512,768]{1,0:T(8,128)(2,1)}) %reduce-scatter.9.cloned.1.call-update) | async-done | bytes 786448 | tf_op jit(solution)/shard_map/reduce_scatter | solution.py:248
  313.5 3.0 fusion.69
  316.5 2.2 fusion.120
  321.0 28.6 %all-gather.11.cloned.1.call-done = bf16[2048,768]{1,0:T(8,128)(2,1)} async-done(((bf16[512,768]{1,0:T(8,128)(2,1)}), bf16[2048,768]{1,0:T(8,128)(2,1)}) %all-gather.11.cloned.1.call-update) | async-done | bytes 3145744 | tf_op jit(solution)/shard_map/all_gather | solution.py:258
  349.7 3.9 convolution_convert_fusion.5
  353.6 3.3 reshape.260
  360.8 69.2 %while.27 = (s32[]{:T(128)}, bf16[4,2,256,3,64]{2,1,0,4,3:T(2,128)(2,1)}, bf16[4,2,256,3,64]{2,1,0,4,3:T(2,128)(2,1)}, bf16[4,2,256,3,64]{2,1,0,4,3:T(2,128)(2,1...) while((s32[]{:T(128)}, ...), condition=%wide.region_18.19_spmd, body=%wide.region_16.18_spmd.sunk | while | flops 257789440 | bytes 21261944 | solution.py:262
  361.0 2.7 subtract_exponential_fusion.2
  364.8 2.5 fusion.187
  367.3 3.5 fusion.190
  373.8 3.5 fusion.188
  378.3 2.7 subtract_exponential_fusion.2
  382.1 2.5 fusion.187
  384.6 3.5 fusion.190
  388.1 1.8 fusion.189
  391.1 3.5 fusion.188
  395.6 2.7 subtract_exponential_fusion.2
  399.4 2.5 fusion.187
  401.9 3.5 fusion.190
  405.4 1.8 fusion.189
  408.4 3.4 fusion.188
  412.9 2.7 subtract_exponential_fusion.2
  416.7 2.5 fusion.187
  419.2 3.5 fusion.190
  422.7 1.8 fusion.189
  425.7 3.4 fusion.188
  430.0 3.1 reshape.263
  433.1 3.2 reshape.262
  436.3 3.3 reshape.261
  439.7 2.3 fusion.83
  443.1 2.8 add_convert_fusion
  446.1 7.1 convolution_bitcast_fusion
  453.1 4.1 convolution_bitcast_fusion.1
  466.6 17.5 %reduce-scatter.11.cloned.1.call-done = bf16[512,768]{1,0:T(8,128)(2,1)} async-done(((bf16[2048,768]{1,0:T(8,128)(2,1)}), bf16[512,768]{1,0:T(8,128)(2,1)}) %reduce-scatter.11.cloned.1.call-update) | async-done | bytes 786448 | tf_op jit(solution)/shard_map/reduce_scatter | solution.py:282
  484.1 1.8 convert_reduce_fusion.1
  489.5 1.8 select_reduce_fusion.1
  493.4 3.3 fusion.101
  498.8 22.7 %psum.139 = f32[1,768]{1,0:T(1,128)} all-reduce(f32[1,768]{1,0:T(1,128)S(1)} %stack.33), channel_id=1, replica_groups=mesh['rows'=8,'heads'=4] {'rows'}, use_global_device_ids=true, to_apply=%region_48.49 | all-reduce | flops 768 | bytes 6144 | tf_op jit(solution)/shard_map/psum | solution.py:335
  521.5 41.5 %all-reduce.6 = (f32[768]{0:T(1024)}, f32[1,768]{1,0:T(1,128)}, f32[1,768]{1,0:T(1,128)}, f32[1,768]{1,0:T(1,128)}, f32[1,768]{1,0:T(1,128)}, /*index=5*/f32[1,768]{1,0:T(1,128)}, f32[96]{0:T(128)}) all-reduce(f32[768]{0:T(1024)S(1)} %get-tuple-element.235, ...), channel_id=1, replica_groups=mesh['rows'=8,'heads'=4] {'rows','heads'}, use_global_device_ids=true, to_apply=%region_27.28 | all-reduce | flops 4704 | bytes 37632 | tf_op jit(solution)/shard_map/psum | solution.py:350
  564.0 165.1 %all-reduce.14.cloned.1.call-done = (f32[1,768,192]{1,2,0:T(8,128)}, f32[1,768,192]{1,2,0:T(8,128)}, f32[1,768,192]{1,2,0:T(8,128)}, f32[1,192,768]{2,1,0:T(8,12...) async-done(((f32[1,768,192]{1,2,0:T(8,128)}, f32[1,768,192]{1,2,0:T(8,128)}, f32[1,768,192]{1,2,0:T(8,128)}, f32[1,192,768]{2,1,0:T(8,128)}, f32[1,768,768]{2,1,0:T(8,128)}, ...) | async-done | bytes 7077904 | tf_op jit(solution)/shard_map/psum | solution.py:335
  729.1 152.3 %all-reduce.12.cloned.1.call-done = (f32[48,768]{1,0:T(8,128)}, f32[256,768]{1,0:T(8,128)}, f32[1000,768]{1,0:T(8,128)}, f32[768,96]{0,1:T(8,128)}) async-done(((f32[48,768]{1,0:T(8,128)}, f32[256,768]{1,0:T(8,128)}, f32[1000,768]{1,0:T(8,128)}, f32[768,96]{0,1:T(8,128)}), (f32[48,768]{1,0:T(8,128)}, f32[256,768]{1,0:T(8,128)}, f32[1000,768]{1,0:T(8,128)}, ...) | async-done | bytes 4300816 | tf_op jit(solution)/shard_map/psum | solution.py:350
  882.9 2.1 copy.162
  885.0 3.8 copy.163
  (300 shorter events, 86.9 us)
Async XLA Ops:
  7.2 3.9 copy-start
  7.2 3.5 copy-start.23
  7.2 3.5 copy-start.36
  7.2 38.5 %all-gather.5.cloned.1.call-start = ((), (), s32[]{:S(2)}) async-start(), calls=%async_computation.4 | async-start | bytes 3932160 | tf_op jit(solution)/shard_map/all_gather | solution.py:158
  9.2 1.8 copy-start.59
  13.1 1.5 copy-start.44
  13.1 32.6 %copy-start.40 = (bf16[1,768,192]{1,2,0:T(8,128)(2,1)S(1)}, bf16[1,768,192]{1,2,0:T(8,128)(2,1)}, u32[]{:S(2)}) copy-start(bf16[1,768,192]{1,2,0:T(8,128)(2,1)} %param.38) | copy-start | bytes 884740
  14.3 114.5 %reduce-scatter.5.cloned.1.call-start = ((), (), s32[]{:S(2)}) async-start(), calls=%async_computation.5 | async-start | bytes 3932160 | tf_op jit(solution)/shard_map/reduce_scatter | solution.py:167
  48.8 2.8 copy-start.33
  55.5 5.5 copy-start.31
  85.5 2.5 copy-start.38
  90.7 70.6 %all-gather.7.cloned.1.call-start = ((), (), s32[]{:S(2)}) async-start(), calls=%async_computation.6 | async-start | bytes 3932160 | tf_op jit(solution)/shard_map/all_gather | solution.py:172
  130.2 1.1 copy-start.2
  131.3 1.5 copy-start.47
  132.6 91.2 %reduce-scatter.7.cloned.1.call-start = ((), (), s32[]{:S(2)}) async-start(), calls=%async_computation.7 | async-start | bytes 3932160 | tf_op jit(solution)/shard_map/reduce_scatter | solution.py:178
  161.3 20.5 %copy-start.57 = (bf16[1,768,768]{2,1,0:T(8,128)(2,1)S(1)}, bf16[1,768,768]{2,1,0:T(8,128)(2,1)}, u32[]{:S(2)}) copy-start(bf16[1,768,768]{2,1,0:T(8,128)(2,1)} %param.44) | copy-start | bytes 3538948
  180.1 1.7 copy-start.60
  185.7 72.8 %all-gather.9.cloned.1.call-start = ((), (), s32[]{:S(2)}) async-start(), calls=%async_computation.8 | async-start | bytes 3932160 | tf_op jit(solution)/shard_map/all_gather | solution.py:241
  186.7 38.9 %copy-start.24 = (bf16[768,96]{0,1:T(8,128)(2,1)S(1)}, bf16[768,96]{0,1:T(8,128)(2,1)}, u32[]{:S(2)}) copy-start(bf16[768,96]{0,1:T(8,128)(2,1)} %param.46) | copy-start | bytes 442372
  186.7 39.3 %copy-start.55 = (f32[96]{0:T(128)S(1)}, f32[96]{0:T(128)}, u32[]{:S(2)}) copy-start(f32[96]{0:T(128)} %param.47) | copy-start | bytes 1156
  225.6 4.2 copy-start.16
  225.6 1.0 copy-start.29
  229.8 83.7 %reduce-scatter.9.cloned.1.call-start = ((), (), s32[]{:S(2)}) async-start(), calls=%async_computation.9 | async-start | bytes 3932160 | tf_op jit(solution)/shard_map/reduce_scatter | solution.py:248
  258.5 12.8 %copy-start.58 = (bf16[1,768,768]{2,1,0:T(8,128)(2,1)S(1)}, bf16[1,768,768]{2,1,0:T(8,128)(2,1)}, u32[]{:S(2)}) copy-start(bf16[1,768,768]{2,1,0:T(8,128)(2,1)} %param.42) | copy-start | bytes 3538948
  269.6 1.7 copy-start.61
  275.4 74.3 %all-gather.11.cloned.1.call-start = ((), (), s32[]{:S(2)}) async-start(), calls=%async_computation.10 | async-start | bytes 3932160 | tf_op jit(solution)/shard_map/all_gather | solution.py:258
  313.5 3.0 copy-start.20
  316.5 3.4 copy-start.6
  318.6 1.2 copy-start.8
  319.9 29.8 %copy-start.39 = (bf16[1,192,768]{2,1,0:T(8,128)(2,1)S(1)}, bf16[1,192,768]{2,1,0:T(8,128)(2,1)}, u32[]{:S(2)}) copy-start(bf16[1,192,768]{2,1,0:T(8,128)(2,1)} %param.39) | copy-start | bytes 884740
  321.0 163.1 %reduce-scatter.11.cloned.1.call-start = ((), (), s32[]{:S(2)}) async-start(), calls=%async_computation.11 | async-start | bytes 3932160 | tf_op jit(solution)/shard_map/reduce_scatter | solution.py:282
  433.1 6.5 copy-start.32
  439.6 2.3 copy-start.12
  439.6 2.3 copy-start.34
  441.9 1.1 copy-start.14
  441.9 1.2 copy-start.41
  446.0 283.1 %all-reduce.14.cloned.1.call-start = ((), (), s32[]{:S(2)}) async-start(), calls=%async_computation.13 | async-start | bytes 14155776 | tf_op jit(solution)/shard_map/psum | solution.py:335
  446.0 7.1 copy-start.56
  446.0 7.1 copy-start.62
  453.1 4.1 copy-start.19
  457.3 2.1 copy-start.5
  457.3 2.3 copy-start.15
  459.6 1.6 copy-start.11
  461.2 1.6 copy-start.13
  464.4 1.2 copy-start.17
  464.5 416.9 %all-reduce.12.cloned.1.call-start = ((), (), s32[]{:S(2)}) async-start(), calls=%async_computation.12 | async-start | bytes 8601600 | tf_op jit(solution)/shard_map/psum | solution.py:350
  484.1 1.9 copy-start.18
  484.1 2.8 copy-start.9
  485.9 1.4 copy-start.7
  488.1 1.1 copy-start.3
  489.4 1.9 copy-start.4
  496.7 2.1 copy-start.46
  496.7 24.8 %copy-start.43 = (f32[768]{0:T(1024)S(1)}, f32[768]{0:T(1024)}, u32[]{:S(2)}) copy-start(f32[768]{0:T(1024)} %get-tuple-element.173) | copy-start | bytes 9220
  496.7 24.8 %copy-start.42 = (f32[768]{0:T(1024)S(1)}, f32[768]{0:T(1024)}, u32[]{:S(2)}) copy-start(f32[768]{0:T(1024)} %get-tuple-element.177) | copy-start | bytes 9220
  496.7 66.3 %copy-start.30 = (f32[512,48]{0,1:T(8,128)S(1)}, f32[512,48]{0,1:T(8,128)}, u32[]{:S(2)}) copy-start(f32[512,48]{0,1:T(8,128)} %param.48) | copy-start | bytes 294916
  496.7 66.3 %copy-start.37 = (bf16[48,768]{1,0:T(8,128)(2,1)S(1)}, bf16[48,768]{1,0:T(8,128)(2,1)}, u32[]{:S(2)}) copy-start(bf16[48,768]{1,0:T(8,128)(2,1)} %param.30) | copy-start | bytes 221188
  885.0 3.8 copy-start.28
  885.0 4.6 copy-start.27
  888.8 1.6 copy-start.26
  888.8 2.5 copy-start.25
  889.6 2.5 copy-start.22
  892.1 2.5 copy-start.21
  892.1 4.6 copy-start.1
  894.6 1.4 copy-start.35
  (9 other events, 6.6 us)
Sparse Core Ops, SparseCore 0:
  14.5 31.2 all-gather.4
  90.8 37.9 reduce-scatter.4
  132.7 28.5 all-gather.6
  185.8 37.9 reduce-scatter.6
  229.9 28.5 all-gather.8
  275.5 37.9 reduce-scatter.8
  321.1 28.5 all-gather.10
  446.1 37.9 reduce-scatter.10
  490.3 238.7 all-reduce.13
  737.9 143.3 all-reduce.11
where the time goes:
time: 908 us; the launch traced here: 904 us
  waiting for transfers between devices  564 us (62%)
  matrix products  154 us (17%)
  local copies, waits for them, and re-layouts  78.6 us (9%)
  blocking collectives  64.2 us (7%)
  other arithmetic  26.4 us (3%)
  between operations  15.1 us (2%)
    psum x1, waiting for transfers between devices, per_device(): lax.psum((stacked(0), stacked(1), stacked(2), stacked(3), stacked(4), sta...  165 us
    psum x1, waiting for transfers between devices, per_device(): lax.psum((grad_w_in, grad_b_in, grad_pos, grad_cls, stacked(7), stacked(8...  152 us
    psum x1, blocking collectives, per_device(): lax.psum((grad_w_in, grad_b_in, grad_pos, grad_cls, stacked(7), stacked(8...  41.5 us
    dot_general x10, matrix products, matmul(): return jnp.dot(matrix, other, preferred_element_type=jnp.float32)  39.8 us
    reduce_scatter x1, waiting for transfers between devices, per_device(): lax.psum_scatter(matmul_nt(grad_pre, full_up).astype(jnp.bfloat16), 'head...  37.7 us
    reduce_scatter x1, waiting for transfers between devices, per_device(): lax.psum_scatter(matmul(attended, weight_out).astype(jnp.bfloat16), 'head...  37.4 us
    reduce_scatter x1, waiting for transfers between devices, per_device(): lax.psum_scatter(matmul(activated, full_down).astype(jnp.bfloat16), 'head...  37.1 us
    all_gather x1, waiting for transfers between devices, per_device(): rows_norm = lax.all_gather(normed1, 'heads', axis=0, tiled=True)  31.1 us
  transfers between devices with their start and end apart: 10, of which 10 were waited for; matrix products, arithmetic and copies ran while one was open for 4% of the time, Pallas kernels for 0%

commit v1 on v0

--- a/solution.py
+++ b/solution.py
@@ -348,20 +348,23 @@
         sum_w_out,
         sum_b_out,
     ) = lax.psum(
-        (
-            grad_w_in,
-            grad_b_in,
-            grad_pos,
-            grad_cls,
-            stacked(7),
-            stacked(8),
-            stacked(9),
-            stacked(10),
-            stacked(11),
-            grad_w_out,
-            grad_b_out,
+        lax.psum(
+            (
+                grad_w_in,
+                grad_b_in,
+                grad_pos,
+                grad_cls,
+                stacked(7),
+                stacked(8),
+                stacked(9),
+                stacked(10),
+                stacked(11),
+                grad_w_out,
+                grad_b_out,
+            ),
+            "heads",
         ),
-        ("rows", "heads"),
+        "rows",
     )
     return (
         latents,

time: 908 us -> 963 us (1.061)
  waiting for transfers between devices: 564 us -> 647 us
  blocking collectives: 64.2 us -> 49.9 us
  matrix products: 154 us -> 144 us
    psum x1, waiting for transfers between devices: 165 us -> 312 us  [per_device(): lax.psum(lax.psum((grad_w_in, grad_b_in, grad_pos, grad_cls, stacked(7),...]
    psum x1, waiting for transfers between devices: 152 us -> 69.4 us  [per_device(): lax.psum((grad_w_in, grad_b_in, grad_pos, grad_cls, stacked(7), stacked(8...]
    psum x1, blocking collectives: 41.5 us -> 10.2 us  [per_device(): lax.psum((grad_w_in, grad_b_in, grad_pos, grad_cls, stacked(7), stacked(8...]
    reduce_scatter x1, waiting for transfers between devices: 17.5 us -> 35.9 us  [per_device(): lax.psum_scatter((total + matmul_nt(grad_value, weight_value)).astype(jnp...]
    psum x1, blocking collectives: 22.7 us -> 39.7 us  [per_device(): lax.psum(lax.psum((grad_w_in, grad_b_in, grad_pos, grad_cls, stacked(7),...]
    unnamed x138 -> x158, local copies, waits for them, and re-layouts: 26.7 us -> 25.5 us
  transfers between devices with their start and end apart: 10 -> 10, of which waited for: 10 -> 10; matrix products, arithmetic and copies ran while one was open for 4% -> 2% of each run, Pallas kernels for 0% -> 0%
where the time goes in v1:
time: 963 us; the launch traced here: 959 us
  waiting for transfers between devices  647 us (67%)
  matrix products  144 us (15%)
  local copies, waits for them, and re-layouts  74.1 us (8%)
  blocking collectives  49.9 us (5%)
  other arithmetic  27.7 us (3%)
  between operations  15.2 us (2%)
    psum x1, waiting for transfers between devices, per_device(): lax.psum(lax.psum((grad_w_in, grad_b_in, grad_pos, grad_cls, stacked(7),...  312 us
    psum x1, waiting for transfers between devices, per_device(): lax.psum((grad_w_in, grad_b_in, grad_pos, grad_cls, stacked(7), stacked(8...  69.4 us
    dot_general x10, matrix products, matmul(): return jnp.dot(matrix, other, preferred_element_type=jnp.float32)  39.7 us
    psum x1, blocking collectives, per_device(): lax.psum(lax.psum((grad_w_in, grad_b_in, grad_pos, grad_cls, stacked(7),...  39.7 us
    reduce_scatter x1, waiting for transfers between devices, per_device(): lax.psum_scatter(matmul_nt(grad_pre, full_up).astype(jnp.bfloat16), 'head...  37.6 us
    reduce_scatter x1, waiting for transfers between devices, per_device(): lax.psum_scatter(matmul(attended, weight_out).astype(jnp.bfloat16), 'head...  37.4 us
    reduce_scatter x1, waiting for transfers between devices, per_device(): lax.psum_scatter(matmul(activated, full_down).astype(jnp.bfloat16), 'head...  37.3 us
    reduce_scatter x1, waiting for transfers between devices, per_device(): lax.psum_scatter((total + matmul_nt(grad_value, weight_value)).astype(jnp...  35.9 us
  transfers between devices with their start and end apart: 10, of which 10 were waited for; matrix products, arithmetic and copies ran while one was open for 2% of the time, Pallas kernels for 0%

profile of v1, /device:TPU:0, one launch (start us, length us, event | category | flops | bytes accessed | tf_op | source)
XLA Modules:
  0.0 958.9 jit_solution(10851355380793078857)
XLA Ops:
  15.6 31.1 %all-gather.5.cloned.1.call-done = bf16[2048,768]{1,0:T(8,128)(2,1)} async-done(((bf16[512,768]{1,0:T(8,128)(2,1)}), bf16[2048,768]{1,0:T(8,128)(2,1)}) %all-gather.5.cloned.1.call-update) | async-done | bytes 3145744 | tf_op jit(solution)/shard_map/all_gather | solution.py:158
  46.7 3.9 convolution_convert_fusion.6
  50.7 2.6 reshape.258
  54.3 3.9 convolution_convert_fusion.7
  58.3 2.6 reshape.257
  61.9 3.0 convolution_convert_fusion.8
  69.0 12.9 %while.26 = (s32[]{:T(128)}, bf16[4,2,256,3,64]{2,1,0,4,3:T(2,128)(2,1)}, f32[4,2,3,256,1]{3,2,1,4,0:T(4,128)S(1)}, bf16[4,2,256,3,64]{2,4,3,1,0:T(8,128)(2,1)S(...) while((s32[]{:T(128)}, ...), condition=%wide.region_7.8_spmd, body=%wide.region_4.7_spmd.sunk | while | flops 103840256 | bytes 6358125 | solution.py:162
  82.8 2.5 reshape.259
  85.3 2.7 convolution_convert_fusion.4
  88.8 37.4 %reduce-scatter.5.cloned.1.call-done = bf16[512,768]{1,0:T(8,128)(2,1)} async-done(((bf16[2048,768]{1,0:T(8,128)(2,1)}), bf16[512,768]{1,0:T(8,128)(2,1)}) %reduce-scatter.5.cloned.1.call-update) | async-done | bytes 786448 | tf_op jit(solution)/shard_map/reduce_scatter | solution.py:167
  130.3 28.4 %all-gather.7.cloned.1.call-done = bf16[2048,768]{1,0:T(8,128)(2,1)} async-done(((bf16[512,768]{1,0:T(8,128)(2,1)}), bf16[2048,768]{1,0:T(8,128)(2,1)}) %all-gather.7.cloned.1.call-update) | async-done | bytes 3145744 | tf_op jit(solution)/shard_map/all_gather | solution.py:172
  158.6 18.7 %multiply_convert_fusion.1 = (bf16[2048,768]{1,0:T(8,128)(2,1)S(1)}, f32[2048,768]{1,0:T(8,128)}, f32[2048,768]{1,0:T(8,128)}) fusion(f32[768]{0:T(1024)S(1)} %convert_reduce_fusion.6, bf16[2048,768]{1,0:T(8,128)(2,1)} %all-gather.7.cloned.1.call-done, bf16[1,768,768]{2,1,0:T(8,128)(2,1)} %param.42), kind=kOutput, calls=%fused_computation.70 | convolution fusion | flops 2519728128 | bytes 20057088 | tf_op jit(solution)/shard_map/dot_general | solution.py:23
  177.4 1.7 copy-done.71
  179.1 3.9 convolution_convert_fusion.3
  183.9 37.3 %reduce-scatter.7.cloned.1.call-done = bf16[512,768]{1,0:T(8,128)(2,1)} async-done(((bf16[2048,768]{1,0:T(8,128)(2,1)}), bf16[512,768]{1,0:T(8,128)(2,1)}) %reduce-scatter.7.cloned.1.call-update) | async-done | bytes 786448 | tf_op jit(solution)/shard_map/reduce_scatter | solution.py:178
  221.2 1.8 add_convert_fusion.2
  225.4 1.8 fusion.125
  227.2 28.6 %all-gather.9.cloned.1.call-done = bf16[2048,768]{1,0:T(8,128)(2,1)} async-done(((bf16[512,768]{1,0:T(8,128)(2,1)}), bf16[2048,768]{1,0:T(8,128)(2,1)}) %all-gather.9.cloned.1.call-update) | async-done | bytes 3145744 | tf_op jit(solution)/shard_map/all_gather | solution.py:241
  255.8 11.1 %convert_reduce_fusion = (f32[768]{0:T(1024)}, bf16[2048,768]{1,0:T(8,128)(2,1)S(1)}) fusion(f32[2048,768]{1,0:T(8,128)} %get-tuple-element.252, bf16[2048,768]{1,0:T(8,128)(2,1)} %all-gather.9.cloned.1.call-done, bf16[1,768,768]{2,1,0:T(8,128)(2,1)} %param.44, f32[2048,768]{1,0:T(8,128)} %get-tuple-element.267, f32[768]{0:T(1024)S(1)} %copy-done.58), kind=kOutput, calls=%fused_computation.67 | convolution fusion | flops 2442657024 | bytes 20060160 | tf_op jit(solution)/shard_map/dot_general | solution.py:33
  267.0 1.7 copy-done.72
  268.7 4.0 convolution_convert_fusion.2
  273.2 37.6 %reduce-scatter.9.cloned.1.call-done = bf16[512,768]{1,0:T(8,128)(2,1)} async-done(((bf16[2048,768]{1,0:T(8,128)(2,1)}), bf16[512,768]{1,0:T(8,128)(2,1)}) %reduce-scatter.9.cloned.1.call-update) | async-done | bytes 786448 | tf_op jit(solution)/shard_map/reduce_scatter | solution.py:248
  310.9 3.0 fusion.69
  313.8 2.2 fusion.120
  318.3 28.6 %all-gather.11.cloned.1.call-done = bf16[2048,768]{1,0:T(8,128)(2,1)} async-done(((bf16[512,768]{1,0:T(8,128)(2,1)}), bf16[2048,768]{1,0:T(8,128)(2,1)}) %all-gather.11.cloned.1.call-update) | async-done | bytes 3145744 | tf_op jit(solution)/shard_map/all_gather | solution.py:258
  347.0 3.9 convolution_convert_fusion.5
  350.9 2.6 reshape.260
  357.5 60.1 %while.27 = (s32[]{:T(128)}, bf16[4,2,256,3,64]{2,1,0,4,3:T(2,128)(2,1)}, bf16[4,2,256,3,64]{2,1,0,4,3:T(2,128)(2,1)}, bf16[4,2,256,3,64]{2,1,0,4,3:T(2,128)(2,1...) while((s32[]{:T(128)}, ...), condition=%wide.region_18.19_spmd, body=%wide.region_16.18_spmd.sunk | while | flops 257789440 | bytes 27550896 | solution.py:262
  357.8 1.6 subtract_exponential_fusion.2
  360.9 2.5 fusion.187
  363.4 3.5 fusion.190
  366.9 3.5 fusion.188
  372.8 1.6 subtract_exponential_fusion.2
  375.9 2.5 fusion.187
  378.4 3.5 fusion.190
  381.9 3.5 fusion.188
  390.9 2.5 fusion.187
  393.4 3.5 fusion.190
  396.9 3.5 fusion.188
  402.9 1.6 subtract_exponential_fusion.2
  406.0 2.5 fusion.187
  408.5 3.5 fusion.190
  412.0 3.5 fusion.188
  417.5 3.1 reshape.263
  420.7 2.5 reshape.261
  423.2 3.6 reshape.262
  426.8 2.2 fusion.83
  430.2 2.8 add_convert_fusion
  435.2 35.9 %reduce-scatter.11.cloned.1.call-done = bf16[512,768]{1,0:T(8,128)(2,1)} async-done(((bf16[2048,768]{1,0:T(8,128)(2,1)}), bf16[512,768]{1,0:T(8,128)(2,1)}) %reduce-scatter.11.cloned.1.call-update) | async-done | bytes 786448 | tf_op jit(solution)/shard_map/reduce_scatter | solution.py:282
  471.2 1.8 convert_reduce_fusion.1
  476.4 1.7 select_reduce_fusion
  479.4 3.1 fusion.101
  482.8 7.1 convolution_bitcast_fusion
  489.9 4.1 convolution_bitcast_fusion.1
  494.1 1.6 convolution_bitcast_fusion.5
  496.4 1.6 convolution_bitcast_fusion.2
  498.0 1.6 convolution_bitcast_fusion.4
  499.7 1.6 convolution_bitcast_fusion.3
  501.3 69.4 %all-reduce.15.cloned.1.call-done = (f32[48,768]{1,0:T(8,128)}, f32[256,768]{1,0:T(8,128)}, f32[1000,768]{1,0:T(8,128)}, f32[768,96]{0,1:T(8,128)}) async-done(((f32[48,768]{1,0:T(8,128)}, f32[256,768]{1,0:T(8,128)}, f32[1000,768]{1,0:T(8,128)}, f32[768,96]{0,1:T(8,128)}), (f32[48,768]{1,0:T(8,128)}, f32[256,768]{1,0:T(8,128)}, f32[1000,768]{1,0:T(8,128)}, ...) | async-done | bytes 4300816 | tf_op jit(solution)/shard_map/psum | solution.py:351
  573.5 10.2 %all-reduce.8 = (f32[768]{0:T(1024)S(1)}, f32[1,768]{1,0:T(1,128)S(1)}, f32[1,768]{1,0:T(1,128)S(1)}, f32[1,768]{1,0:T(1,128)S(1)}, f32[1,768]{1,0:T(1,128)S(1)}, /*index=5*/f32[1,768]{1,0:T(1,128)S(1)}, f32[96]{0:T(128)S(1)}) all-reduce(f32[768]{0:T(1024)S(1)} %get-tuple-element.247, ...), channel_id=1, replica_groups=mesh['rows'=8,'heads'=4] {'heads'}, use_global_device_ids=true, to_apply=%region_28.29 | all-reduce | flops 4704 | bytes 37632 | tf_op jit(solution)/shard_map/psum | solution.py:351
  583.7 39.7 %all-reduce.6 = (f32[768]{0:T(1024)}, f32[1,768]{1,0:T(1,128)}, f32[1,768]{1,0:T(1,128)}, f32[1,768]{1,0:T(1,128)}, f32[1,768]{1,0:T(1,128)}, /*index=5*/f32[1,768]{1,0:T(1,128)}, f32[1,768]{1,0:T(1,128)}, f32[96]{0:T(128)}) all-reduce(f32[768]{0:T(1024)S(1)} %get-tuple-element.234, ...), channel_id=1, replica_groups=mesh['rows'=8,'heads'=4] {'rows'}, use_global_device_ids=true, to_apply=%region_29.30 | all-reduce | flops 5472 | bytes 43776 | tf_op jit(solution)/shard_map/psum | solution.py:350
  624.4 312.1 %all-reduce.13.cloned.1.call-done = (f32[48,768]{1,0:T(8,128)}, f32[256,768]{1,0:T(8,128)}, f32[1000,768]{1,0:T(8,128)}, f32[1,768,192]{1,2,0:T(8,128)}, f32[1,7...) async-done(((f32[48,768]{1,0:T(8,128)}, ...) | async-done | bytes 11378704 | tf_op jit(solution)/shard_map/psum | solution.py:350
  938.1 2.1 copy.166
  940.1 3.8 copy.167
  (328 shorter events, 82.2 us)
Async XLA Ops:
  7.2 5.3 copy-start
  7.2 4.9 copy-start.26
  7.2 4.9 copy-start.39
  7.2 39.5 %all-gather.5.cloned.1.call-start = ((), (), s32[]{:S(2)}) async-start(), calls=%async_computation.4 | async-start | bytes 3932160 | tf_op jit(solution)/shard_map/all_gather | solution.py:158
  10.6 1.8 copy-start.70
  14.1 1.5 copy-start.54
  14.1 32.6 %copy-start.34 = (bf16[1,768,192]{1,2,0:T(8,128)(2,1)S(1)}, bf16[1,768,192]{1,2,0:T(8,128)(2,1)}, u32[]{:S(2)}) copy-start(bf16[1,768,192]{1,2,0:T(8,128)(2,1)} %param.37) | copy-start | bytes 884740
  15.3 110.8 %reduce-scatter.5.cloned.1.call-start = ((), (), s32[]{:S(2)}) async-start(), calls=%async_computation.5 | async-start | bytes 3932160 | tf_op jit(solution)/shard_map/reduce_scatter | solution.py:167
  50.7 3.7 copy-start.36
  58.3 3.7 copy-start.43
  82.8 2.5 copy-start.41
  85.3 2.7 copy-start.11
  88.1 70.6 %all-gather.7.cloned.1.call-start = ((), (), s32[]{:S(2)}) async-start(), calls=%async_computation.6 | async-start | bytes 3932160 | tf_op jit(solution)/shard_map/all_gather | solution.py:172
  127.9 2.0 copy-start.49
  128.7 1.5 copy-start.59
  130.0 91.2 %reduce-scatter.7.cloned.1.call-start = ((), (), s32[]{:S(2)}) async-start(), calls=%async_computation.7 | async-start | bytes 3932160 | tf_op jit(solution)/shard_map/reduce_scatter | solution.py:178
  130.3 47.1 %copy-start.57 = (f32[768]{0:T(1024)}, f32[768]{0:T(1024)S(1)}, u32[]{:S(2)}) copy-start(f32[768]{0:T(1024)S(1)} %convert_reduce_fusion.6) | copy-start | bytes 9220
  130.3 48.8 %copy-start.68 = (bf16[1,768,768]{2,1,0:T(8,128)(2,1)S(1)}, bf16[1,768,768]{2,1,0:T(8,128)(2,1)}, u32[]{:S(2)}) copy-start(bf16[1,768,768]{2,1,0:T(8,128)(2,1)} %param.44) | copy-start | bytes 3538948
  177.4 1.7 copy-start.71
  183.0 72.8 %all-gather.9.cloned.1.call-start = ((), (), s32[]{:S(2)}) async-start(), calls=%async_computation.8 | async-start | bytes 3932160 | tf_op jit(solution)/shard_map/all_gather | solution.py:241
  183.9 39.1 %copy-start.27 = (bf16[768,96]{0,1:T(8,128)(2,1)S(1)}, bf16[768,96]{0,1:T(8,128)(2,1)}, u32[]{:S(2)}) copy-start(bf16[768,96]{0,1:T(8,128)(2,1)} %param.46) | copy-start | bytes 442372
  183.9 39.5 %copy-start.65 = (f32[96]{0:T(128)S(1)}, f32[96]{0:T(128)}, u32[]{:S(2)}) copy-start(f32[96]{0:T(128)} %param.47) | copy-start | bytes 1156
  223.0 4.2 copy-start.19
  223.0 2.3 copy-start.66
  225.3 30.5 %copy-start.58 = (f32[768]{0:T(1024)S(1)}, f32[768]{0:T(1024)}, u32[]{:S(2)}) copy-start(f32[768]{0:T(1024)} %copy-done.57) | copy-start | bytes 9220
  227.2 83.7 %reduce-scatter.9.cloned.1.call-start = ((), (), s32[]{:S(2)}) async-start(), calls=%async_computation.9 | async-start | bytes 3932160 | tf_op jit(solution)/shard_map/reduce_scatter | solution.py:248
  255.8 12.8 %copy-start.69 = (bf16[1,768,768]{2,1,0:T(8,128)(2,1)S(1)}, bf16[1,768,768]{2,1,0:T(8,128)(2,1)}, u32[]{:S(2)}) copy-start(bf16[1,768,768]{2,1,0:T(8,128)(2,1)} %param.42) | copy-start | bytes 3538948
  267.0 1.7 copy-start.72
  272.7 38.1 %copy-start.46 = (f32[512]{0:T(512)S(1)}, f32[512]{0:T(512)}, u32[]{:S(2)}) copy-start(f32[512]{0:T(512)} %copy-done.45) | copy-start | bytes 6148
  272.7 41.1 %copy-start.50 = (f32[512]{0:T(512)S(1)}, f32[512]{0:T(512)}, u32[]{:S(2)}) copy-start(f32[512]{0:T(512)} %copy-done.49) | copy-start | bytes 6148
  272.7 74.2 %all-gather.11.cloned.1.call-start = ((), (), s32[]{:S(2)}) async-start(), calls=%async_computation.10 | async-start | bytes 3932160 | tf_op jit(solution)/shard_map/all_gather | solution.py:258
  310.9 3.0 copy-start.23
  313.8 3.3 copy-start.7
  317.2 29.8 %copy-start.42 = (bf16[1,192,768]{2,1,0:T(8,128)(2,1)S(1)}, bf16[1,192,768]{2,1,0:T(8,128)(2,1)}, u32[]{:S(2)}) copy-start(bf16[1,192,768]{2,1,0:T(8,128)(2,1)} %param.39) | copy-start | bytes 884740
  318.3 152.9 %reduce-scatter.11.cloned.1.call-start = ((), (), s32[]{:S(2)}) async-start(), calls=%async_computation.11 | async-start | bytes 3932160 | tf_op jit(solution)/shard_map/reduce_scatter | solution.py:282
  420.7 6.1 copy-start.35
  423.2 5.8 copy-start.14
  426.8 2.2 copy-start.37
  433.1 137.7 %all-reduce.15.cloned.1.call-start = ((), (), s32[]{:S(2)}) async-start(), calls=%async_computation.13 | async-start | bytes 8601600 | tf_op jit(solution)/shard_map/psum | solution.py:351
  434.2 38.8 %copy-start.48 = (f32[512]{0:T(512)S(1)}, f32[512]{0:T(512)}, u32[]{:S(2)}) copy-start(f32[512]{0:T(512)} %copy-done.47) | copy-start | bytes 6148
  471.2 1.9 copy-start.21
  471.2 2.8 copy-start.10
  476.4 1.9 copy-start.3
  482.6 453.9 %all-reduce.13.cloned.1.call-start = ((), (), s32[]{:S(2)}) async-start(), calls=%async_computation.12 | async-start | bytes 22757376 | tf_op jit(solution)/shard_map/psum | solution.py:350
  482.8 7.1 copy-start.67
  482.8 7.1 copy-start.73
  489.9 4.1 copy-start.12
  489.9 4.1 copy-start.22
  494.1 2.2 copy-start.6
  494.1 2.4 copy-start.18
  496.4 1.6 copy-start.15
  498.0 1.6 copy-start.16
  570.7 2.7 copy-start.56
  570.7 2.7 copy-start.53
  570.7 2.7 copy-start.52
  570.7 52.7 %copy-start.33 = (f32[512,48]{0,1:T(8,128)S(1)}, f32[512,48]{0,1:T(8,128)}, u32[]{:S(2)}) copy-start(f32[512,48]{0,1:T(8,128)} %param.48) | copy-start | bytes 294916
  570.8 52.7 %copy-start.40 = (bf16[48,768]{1,0:T(8,128)(2,1)S(1)}, bf16[48,768]{1,0:T(8,128)(2,1)}, u32[]{:S(2)}) copy-start(bf16[48,768]{1,0:T(8,128)(2,1)} %param.30) | copy-start | bytes 221188
  940.1 3.8 copy-start.31
  940.1 4.6 copy-start.30
  944.0 1.6 copy-start.29
  944.0 2.5 copy-start.28
  944.8 2.5 copy-start.25
  947.2 2.5 copy-start.24
  947.2 4.6 copy-start.1
  (23 other events, 24.5 us)
Sparse Core Ops, SparseCore 0:
  15.5 31.2 all-gather.4
  88.2 37.9 reduce-scatter.4
  130.1 28.5 all-gather.6
  183.1 37.9 reduce-scatter.6
  227.3 28.5 all-gather.8
  272.9 37.9 reduce-scatter.8
  318.4 28.5 all-gather.10
  433.2 37.9 reduce-scatter.10
  482.7 88.0 all-reduce.14
  577.9 358.5 all-reduce.12
